TPU v7x, 32 devices: a whole 2x2x4 slice. The times are simulated.
32 devices in a mesh: depth: 2 (over core), row: 4 (over y, x), col: 4 (over z).
Axes of the slice: x: 2, y: 2, z: 4, core: 2. Of those that a mesh axis runs over, the one named last changes fastest.
Arguments:
- a_blocks: float32 [32, 8, 4096], P('row', 'col'), may hold values from -0.75 to 0.75
- a_index: int32 [32, 8], P('row', 'col'), may hold values from -1 to 1023, as said below
- b_blocks: float32 [64, 8, 4096], P('col', 'row'), may hold values from -6 to 6
- b_index: int32 [64, 8], P('col', 'row'), may hold values from -1 to 1023, as said below
- c_index: int32 [32, 16], P('row', 'col'), may hold values from -1 to 15, as said below
Outputs:
- c_blocks: float32 [32, 16, 4096], P('row', 'col')
Inputs may be any that keep to these rules, and one draw needn't show every extreme that they name: `a_index`: slots j * 2 to (j + 1) * 2 - 1 of a block row hold block columns of k-panel j, that is j * 256 to (j + 1) * 256 - 1, or -1; the block columns of one row are distinct. Every slot group of some block rows is full. `b_index`: slots i * 2 to (i + 1) * 2 - 1 of a block column hold block rows i * 256 to (i + 1) * 256 - 1, or -1; the block rows of one column are distinct. Every slot group of some block columns is full. `c_index`: the kept block columns of one slot group of a row are distinct. Every slot group of some block rows is full.
All inputs are finite; a program needn't handle non-finite values.
Results may differ from a plain program's by a relative error of at most 0.0003.
Values sent between devices are 32-bit elements; how exact they have to be, the bound alone decides.
No kernel may reach another device: no remote copies, remote signals or barrier semaphores. Data moves between devices by JAX's collectives and lax.ppermute only.
A program may use at most 128 MiB of HBM per device.

v0:
```python
import jax
import jax.numpy as jnp
from jax import lax
from jax.sharding import PartitionSpec as P

BS = 64
KB = 1024


def slot_lookup(indices, table_len):
    matches = indices[:, :, None] == jnp.arange(table_len, dtype=jnp.int32)[None, None, :]
    slot_ids = jnp.arange(indices.shape[1], dtype=jnp.int32)[None, :, None]
    located = jnp.any(matches, axis=1)
    return jnp.where(located, jnp.sum(jnp.where(matches, slot_ids, 0), axis=1), -1)


def per_device(a_blocks, a_index, b_blocks, b_index, c_index):
    rows_dev = a_index.shape[0]
    cols_dev = b_index.shape[0]
    layers = lax.axis_size("depth")
    layer_id = lax.axis_index("depth")
    c_share = c_index.shape[1]
    a_share = a_index.shape[1] // layers
    a_send = lax.dynamic_slice_in_dim(a_blocks, layer_id * a_share, a_share, 1)
    a_ids_send = lax.dynamic_slice_in_dim(a_index, layer_id * a_share, a_share, 1)
    c_valid = c_index >= 0
    c_safe = jnp.where(c_valid, c_index, 0)
    empty = jnp.zeros((rows_dev, c_share, BS, BS), jnp.float32)
    b_whole, b_ids = (
        lax.all_gather(b_blocks, "row", axis=1, tiled=True),
        lax.all_gather(b_index, "row", axis=1, tiled=True),
    )
    b_table = slot_lookup(b_ids, KB)
    b_four = b_whole.reshape(cols_dev, b_ids.shape[1], BS, BS)
    a_part = lax.all_gather(a_send, "col", axis=1, tiled=True)
    a_ids = lax.all_gather(a_ids_send, "col", axis=1, tiled=True)
    slot_count = a_ids.shape[1]
    a_four = a_part.reshape(rows_dev, slot_count, BS, BS)
    k_safe = jnp.where(a_ids >= 0, a_ids, 0)
    u_ids = b_table[c_safe[:, :, None], k_safe[:, None, :]]
    usable = c_valid[:, :, None] & (a_ids >= 0)[:, None, :] & (u_ids >= 0)
    chosen = b_four[c_safe[:, :, None], jnp.where(usable, u_ids, 0)]
    chosen = jnp.where(usable[:, :, :, None, None], chosen, 0.0)
    totals = empty + jnp.einsum("rsac,rtscx->rtax", a_four, chosen, precision=lax.Precision.HIGHEST)
    flattened = totals.reshape(rows_dev, c_share, BS * BS)
    return lax.psum(flattened, "depth")


def solution(mesh):
    placed = (
        P("row", "col", None),
        P("row", "col"),
        P("col", "row", None),
        P("col", "row"),
        P("row", "col"),
    )
    return jax.shard_map(
        per_device, mesh=mesh, in_specs=placed, out_specs=P("row", "col", None), check_vma=False
    )
```

profile of v0, /device:TPU:0, one launch (start us, length us, event | category | flops | bytes accessed | tf_op | source)
XLA Modules:
  0.0 98.5 jit_solution(11997284042724880508)
XLA Ops:
  6.5 2.2 %copy.42 = f32[16,2,4096]{2,0,1:T(8,128)} copy(f32[16,2,4096]{2,1,0:T(2,128)} %param.7) | data formatting | bytes 1048576 | tf_op args[2]
  8.8 0.7 dynamic-slice_bitcast_fusion
  9.5 12.6 %all-gather = s32[4,1,8]{2,1,0:T(1,128)S(1)} all-gather(s32[1,1,8]{2,1,0:T(1,128)S(1)} %dynamic-slice_bitcast_fusion), channel_id=1, replica_groups=mesh['depth'=2,'row'=4,'col'=4] {'col'}, dimensions={0}, use_global_device_ids=true | all-gather | bytes 160 | tf_op jit(solution)/shard_map/all_gather | solution.py:36
  22.2 0.7 fusion.13
  23.1 0.1 reshape.60
  23.2 8.2 %all-gather.1 = s32[4,2,16]{2,1,0:T(2,128)S(1)} all-gather(s32[1,2,16]{2,1,0:T(2,128)} %bitcast.34), channel_id=1, replica_groups=mesh['depth'=2,'row'=4,'col'=4] {'row'}, dimensions={0}, use_global_device_ids=true | all-gather | bytes 640 | tf_op jit(solution)/shard_map/all_gather | solution.py:31
  31.5 0.2 fusion.8
  31.7 0.2 select_reduce_fusion
  32.0 1.5 %gather_fusion = s32[128]{0:T(128)S(1)} fusion(s32[16,1024]{1,0:T(8,128)S(1)} %broadcast_select_fusion, s32[128]{0:T(128)S(1)} %reshape.60), kind=kCustom, calls=%fused_computation | custom fusion | bytes 2048 | tf_op jit(solution)/shard_map/gather | solution.py:40
  33.4 0.1 gather.9
  33.9 0.1 reshape.66
  34.0 0.1 reshape.74
  34.1 0.1 constant_dynamic-slice_fusion
  34.3 14.8 %all_gather.15 = f32[8,4,4096]{2,0,1:T(8,128)S(1)} all-gather(f32[8,1,4096]{2,0,1:T(8,128)S(1)} %copy.52), channel_id=1, replica_groups=mesh['depth'=2,'row'=4,'col'=4] {'col'}, dimensions={1}, use_global_device_ids=true | all-gather | bytes 655360 | tf_op jit(solution)/shard_map/all_gather | solution.py:35
  49.1 0.3 copy.47
  49.5 0.5 reshape.81
  50.1 4.6 %reshape.57 = f32[16,8,64,64]{3,2,0,1:T(8,128)} reshape(f32[16,8,4096]{2,0,1:T(8,128)} %all-gather.4.cloned.1.call-done) | data formatting | bytes 4194304 | tf_op jit(solution)/shard_map/reshape | solution.py:34
  54.7 5.0 %gather_fusion.1 = f32[128,64,64]{2,1,0:T(8,128)} fusion(f32[16,8,64,64]{3,2,0,1:T(8,128)} %reshape.57, s32[128]{0:T(128)S(1)} %reshape.66), kind=kCustom, calls=%fused_computation.1 | custom fusion | bytes 4195328 | tf_op jit(solution)/shard_map/gather | solution.py:42
  59.8 5.6 %copy.45 = f32[128,64,64]{1,2,0:T(8,128)} copy(f32[128,64,64]{2,1,0:T(8,128)} %gather_fusion.1) | data formatting | bytes 4194304 | tf_op jit(solution)/shard_map/gather | solution.py:42
  65.4 5.8 %fusion.4 = f32[8,4,64,64]{2,3,1,0:T(8,128)S(1)} fusion(f32[8,4,4,64,64]{3,4,2,1,0:T(8,128)} %bitcast.30, pred[8,4,4]{2,1,0:T(4,128)(4,1)S(1)} %and_and_fusion, f32[8,4,64,64,1]{3,2,1,0,4:T(8,128)S(1)} %reshape.81), kind=kOutput, calls=%fused_computation.6 | convolution fusion | flops 403177472 | bytes 3145856 | tf_op jit(solution)/shard_map/rsac,rtscx->rtax/dot_general | solution.py:44
  71.2 0.3 copy.48
  71.6 1.2 %reshape.59 = f32[8,4,4096]{2,0,1:T(8,128)} reshape(f32[8,4,64,64]{3,2,0,1:T(8,128)S(1)} %copy.48) | data formatting | bytes 1048576 | tf_op jit(solution)/shard_map/reshape | solution.py:45
  72.7 16.7 %all-reduce.2.cloned.1.call-done = f32[8,4,4096]{2,0,1:T(8,128)} async-done(((f32[8,4,4096]{2,0,1:T(8,128)}), f32[8,4,4096]{2,0,1:T(8,128)}) %all-reduce.2.cloned.1.call-update) | async-done | bytes 524304 | tf_op jit(solution)/shard_map/psum | solution.py:46
  89.5 2.2 %copy.49 = f32[8,4,4096]{2,1,0:T(4,128)} copy(f32[8,4,4096]{2,0,1:T(8,128)} %all-reduce.2.cloned.1.call-done) | data formatting | bytes 1048576 | tf_op jit(solution)/shard_map/psum | solution.py:46
  (23 shorter events, 0.9 us)
Async XLA Ops:
  6.5 27.6 %copy-start = (f32[8,2,4096]{2,1,0:T(2,128)S(1)}, f32[8,2,4096]{2,1,0:T(2,128)}, u32[]{:S(2)}) copy-start(f32[8,2,4096]{2,1,0:T(2,128)} %param.5) | copy-start | bytes 786436
  6.5 43.6 %all-gather.4.cloned.1.call-start = ((), (), s32[]{:S(2)}) async-start(), calls=%async_computation | async-start | bytes 2621440 | tf_op jit(solution)/shard_map/all_gather | solution.py:30
  8.7 80.7 %all-reduce.2.cloned.1.call-start = ((), (), s32[]{:S(2)}) async-start(), calls=%async_computation.1 | async-start | bytes 1048576 | tf_op jit(solution)/shard_map/psum | solution.py:46
  31.9 1.7 %copy-start.1 = (s32[8,4]{0,1:T(4,128)S(1)}, s32[8,4]{0,1:T(4,128)}, u32[]{:S(2)}) copy-start(s32[8,4]{0,1:T(4,128)} %param.9) | copy-start | bytes 388
Sparse Core Ops, SparseCore 0:
  9.2 37.9 all-gather.3
  72.9 16.5 all-reduce.1
where the time goes:
time: 98.9 us; the launch traced here: 98.5 us
  blocking collectives  35.6 us (36%)
  local copies, waits for them, and re-layouts  25.2 us (25%)
  waiting for transfers between devices  16.8 us (17%)
  between operations  13.5 us (14%)
  matrix products  5.82 us (6%)
  other arithmetic  1.43 us (1%)
    psum x1, waiting for transfers between devices, per_device(): return lax.psum(flattened, 'depth')  16.7 us
    all_gather x1, blocking collectives, per_device(): a_part = lax.all_gather(a_send, 'col', axis=1, tiled=True)  14.8 us
    all_gather x1, blocking collectives, per_device(): a_ids = lax.all_gather(a_ids_send, 'col', axis=1, tiled=True)  12.6 us
    gather x2, local copies, waits for them, and re-layouts, per_device(): chosen = b_four[c_safe[:, :, None], jnp.where(usable, u_ids, 0)]  10.7 us
    all_gather x1, blocking collectives, per_device(): lax.all_gather(b_index, 'row', axis=1, tiled=True)  8.22 us
    dot_general x1, matrix products, per_device(): jnp.einsum('rsac,rtscx->rtax', a_four, chosen, precision=lax.Precision.HI...  5.82 us
    reshape x1, local copies, waits for them, and re-layouts, per_device(): b_four = b_whole.reshape(cols_dev, b_ids.shape[1], BS, BS)  4.62 us
    unnamed x8, local copies, waits for them, and re-layouts  3.03 us
  transfers between devices with their start and end apart: 2, of which 1 were waited for; matrix products, arithmetic and copies ran while one was open for 6% of the time, Pallas kernels for 0%

commit v1 on v0

v1 whole, which is shorter than its diff:
```python
import functools

import jax
import jax.numpy as jnp
from jax import lax
from jax.experimental import pallas as pl
from jax.experimental.pallas import tpu as pltpu
from jax.sharding import PartitionSpec as P


BS = 64
LANES = 128
HALF = BS * BS // LANES
AXES = ("depth", "row", "col")
UNROLL = 2
VMEM = pl.BlockSpec(memory_space=pltpu.VMEM)
SMEM = pl.BlockSpec(memory_space=pltpu.SMEM)


def plan(n_row, n_col):
    half, n = n_row // 2, n_col // 2
    ratio = n_col // n_row
    place = lambda d, i, j: (d * n_row + i) * n_col + j
    chips = [(i, j) for i in range(n_row) for j in range(n_col)]
    b_steps = [
        [((d, i, j), (d, i ^ hop, j)) for d, hop in enumerate((k, half + k - 1)) for i, j in chips]
        for k in range(1, half)
    ]
    b_steps.append(
        [((0, i, j), (1, i ^ (n_row - 1), j)) for i, j in chips] + [((1, i, j), (0, i, j)) for i, j in chips]
    )
    a_steps = []
    for r in reversed(range(n)):
        step = []
        for i in range(n_row):
            kinds = [[], []]
            for p in range(n_col):
                kinds[int((p // ratio) ^ i >= half)].append(p)
            for q in range(n):
                for d in (0, 1):
                    here, there = kinds[d][q], kinds[1 - d][q ^ r]
                    if r:
                        step.append(((1 - d, i, here), (d, i, there)))
                        step.append(((d, i, here), (d, i, kinds[d][q ^ r])))
                    else:
                        step.append(((d, i, here), (d, i, there)))
                        step.append(((1 - d, i, here), (d, i, here)))
        a_steps.append(step)
    flat = lambda steps: [[(place(*s), place(*t)) for s, t in step] for step in steps]
    for step in flat(a_steps) + flat(b_steps):
        assert [sorted(x) for x in zip(*step)] == [list(range(2 * n_row * n_col))] * 2
    return flat(a_steps), flat(b_steps)


def rows_of(blocks):
    n, slots, _ = blocks.shape
    return blocks.reshape(n, slots, HALF, LANES).transpose(0, 2, 1, 3).reshape(n * HALF * slots, LANES)


def blocks_of(rows, n, slots):
    return rows.reshape(n, HALF, slots, LANES).transpose(0, 2, 1, 3).reshape(n, slots, HALF * LANES)


def pick(refs, which, row, stride):
    value = refs[0][pl.ds(row, HALF, stride=stride), :]
    for k in range(1, len(refs)):
        value = jnp.where(which == k, refs[k][pl.ds(row, HALF, stride=stride), :], value)
    return value


def packed(fields):
    code, shift = jnp.int32(0), 0
    for value, size in reversed(fields):
        code = code | (value << shift)
        shift += (size - 1).bit_length()
    return code


def unpacked(code, sizes):
    values = []
    for size in reversed(sizes):
        width = (size - 1).bit_length()
        values.append(code & ((1 << width) - 1))
        code = code >> width
    return values[::-1]


def list_kernel(dims, mesh_dims, c_ids, *refs):
    rows, cols, sa, sb, sc = dims
    n_row, n_col = mesh_dims
    n_a, n_b, ratio = n_col // 2, n_row // 2, n_col // n_row
    a_ids, b_ids = refs[:n_a], refs[n_a : n_a + n_b]
    total, entries, out = refs[n_a + n_b :]
    sizes = (rows, sc, cols, n_a, sa, n_b, sb)
    core, i, j = (lax.axis_index(name) for name in AXES)
    out[...] = jnp.zeros_like(out)
    count = jnp.int32(0)
    for x in range(n_b):
        q = i ^ jnp.where(core == 0, (x + 1) % n_b, n_b + x)
        for r in range(ratio):
            which = n_a - 1 - (((q * ratio + r) ^ j) & (n_a - 1))
            for m in range(rows):
                mine = []
                for s in range(sa):
                    k = a_ids[0][s, m]
                    for a in range(1, n_a):
                        k = jnp.where(which == a, a_ids[a][s, m], k)
                    mine.append(jnp.where(k < 0, -2, k))
                for t in range(sc):
                    n = c_ids[t, m]
                    at = jnp.maximum(n, 0)
                    for u in range(sb):
                        k = jnp.where(n < 0, -1, b_ids[x][u, at])
                        slot, hit = jnp.int32(0), k == mine[0]
                        for s in range(1, sa):
                            slot = jnp.where(k == mine[s], s, slot)
                            hit = hit | (k == mine[s])
                        entries[count] = packed(list(zip((m, t, at, which, slot, x, u), sizes)))
                        count = count + hit.astype(jnp.int32)
    for k in range(UNROLL):
        entries[count + k] = 0
    total[0] = count


def product_kernel(dims, n_a, n_b, total, entries, *refs):
    rows, cols, sa, sb, sc = dims
    a_refs, b_refs = refs[:n_a], refs[n_a : n_a + n_b]
    _, out, spread = refs[n_a + n_b :]
    sizes = (rows, sc, cols, n_a, sa, n_b, sb)
    count = total[0]
    low = lax.broadcasted_iota(jnp.int32, (HALF, LANES), 1) < BS

    def one(e, lane):
        m, t, c, a, s, b, u = unpacked(entries[e], sizes)
        x = pick(a_refs, a, m * (sa * HALF) + s, sa)
        x = jnp.where(e < count, x, 0.0)
        y = pick(b_refs, b, c * (sb * HALF) + u, sb)
        turned = pltpu.roll(y, BS, 1)
        wide = spread.at[lane]
        wide[pl.ds(0, HALF, stride=2), :] = jnp.where(low, y, 0.0)
        wide[pl.ds(1, HALF, stride=2), :] = jnp.where(low, turned, 0.0)
        wide[pl.ds(BS, HALF, stride=2), :] = jnp.where(low, 0.0, turned)
        wide[pl.ds(BS + 1, HALF, stride=2), :] = jnp.where(low, 0.0, y)
        w = wide[...]
        x_hi = x.astype(jnp.bfloat16)
        x_lo = (x - x_hi.astype(jnp.float32)).astype(jnp.bfloat16)
        w_hi = w.astype(jnp.bfloat16)
        w_lo = (w - w_hi.astype(jnp.float32)).astype(jnp.bfloat16)
        z = jnp.dot(
            jnp.concatenate([x_hi, x_lo], axis=0),
            jnp.concatenate([w_hi, w_lo], axis=1),
            preferred_element_type=jnp.float32,
        )
        z = (z[:HALF, :LANES] + z[HALF:, :LANES]) + (z[:HALF, LANES:] + z[HALF:, LANES:])
        return m * (sc * HALF) + t, z

    def step(k, carry):
        done = [one(k * UNROLL + lane, lane) for lane in range(UNROLL)]
        for row, z in done:
            where = (pl.ds(row, HALF, stride=sc), slice(None))
            out[where] = out[where] + z
        return carry

    lax.fori_loop(0, (count + UNROLL - 1) // UNROLL, step, 0)


def per_device(n_row, n_col, a_blocks, a_index, b_blocks, b_index, c_index):
    a_steps, b_steps = plan(n_row, n_col)
    dims = (a_index.shape[0], b_index.shape[0], a_index.shape[1], b_index.shape[1], c_index.shape[1])
    rows, _, sa, _, sc = dims
    full = jax.ShapeDtypeStruct((rows * HALF * sc, LANES), jnp.float32)
    cap = rows * sc * sa * (n_col // 2) + UNROLL + 6

    b_list = [rows_of(lax.ppermute(b_blocks, AXES, step)) for step in b_steps]
    a_list = [rows_of(lax.ppermute(a_blocks, AXES, step)) for step in a_steps]
    b_ids = [lax.ppermute(b_index.T, AXES, step) for step in b_steps]
    a_ids = [lax.ppermute(a_index.T, AXES, step) for step in a_steps]
    count, entries, empty = pl.pallas_call(
        functools.partial(list_kernel, dims, (n_row, n_col)),
        out_shape=[jax.ShapeDtypeStruct((1,), jnp.int32), jax.ShapeDtypeStruct((cap,), jnp.int32), full],
        in_specs=[SMEM] * (1 + len(a_ids) + len(b_ids)),
        out_specs=[SMEM, SMEM, VMEM],
        compiler_params=pltpu.CompilerParams(vmem_limit_bytes=16 * 1024 * 1024),
        cost_estimate=pl.CostEstimate(flops=0, bytes_accessed=1_000_000, transcendentals=0),
        name="list",
    )(c_index.T, *a_ids, *b_ids)
    part = pl.pallas_call(
        functools.partial(product_kernel, dims, len(a_list), len(b_list)),
        out_shape=full,
        in_specs=[SMEM] * 2 + [VMEM] * (len(a_list) + len(b_list) + 1),
        out_specs=VMEM,
        scratch_shapes=[pltpu.VMEM((UNROLL, LANES, LANES), jnp.float32)],
        input_output_aliases={2 + len(a_list) + len(b_list): 0},
        compiler_params=pltpu.CompilerParams(vmem_limit_bytes=16 * 1024 * 1024),
        cost_estimate=pl.CostEstimate(flops=100_000_000, bytes_accessed=2_000_000, transcendentals=0),
        name="products",
    )(count, entries, *a_list, *b_list, empty)
    other = lax.ppermute(part, "depth", [(0, 1), (1, 0)])
    return blocks_of(part + other, rows, sc)


def solution(mesh):
    placed = (
        P("row", "col", None),
        P("row", "col"),
        P("col", "row", None),
        P("col", "row"),
        P("row", "col"),
    )
    n_row, n_col = mesh.shape["row"], mesh.shape["col"]

    def body(*args):
        return per_device(n_row, n_col, *args)

    return jax.shard_map(
        body, mesh=mesh, in_specs=placed, out_specs=P("row", "col", None), check_vma=False
    )
```

time: 98.9 us -> 35.8 us (0.36)
  blocking collectives: 35.6 us -> 0 us
  local copies, waits for them, and re-layouts: 25.2 us -> 0.01 us
  starting transfers between devices: 0.04 us -> 14.5 us
  between operations: 13.5 us -> 0.06 us
  matrix products: 5.82 us -> 0 us
  Pallas kernels: 0 us -> 3.53 us
    all_gather x3 -> x0, blocking collectives: 35.6 us -> none  [the longest x1 14.8 us: per_device(): a_part = lax.all_gather(a_send, 'col', axis=1, tiled=True)]
    psum x1 -> x0, waiting for transfers between devices: 16.7 us -> none  [per_device(): return lax.psum(flattened, 'depth')]
    ppermute x0 -> x9, waiting for transfers between devices: none -> 16.7 us  [the longest x2 9.83 us: per_device(): a_ids = [lax.ppermute(a_index.T, AXES, step) for step in a_steps]]
    ppermute x0 -> x9, starting transfers between devices: none -> 14.5 us  [the longest x2 4.17 us: per_device(): a_list = [rows_of(lax.ppermute(a_blocks, AXES, step)) for step in a_steps]]
    gather x4 -> x0, local copies, waits for them, and re-layouts: 12.2 us -> none  [the longest x2 10.7 us: per_device(): chosen = b_four[c_safe[:, :, None], jnp.where(usable, u_ids, 0)]]
    reshape x3 -> x0, local copies, waits for them, and re-layouts: 6.29 us -> none  [the longest x1 4.62 us: per_device(): b_four = b_whole.reshape(cols_dev, b_ids.shape[1], BS, BS)]
    dot_general x1 -> x0, matrix products: 5.82 us -> none  [per_device(): jnp.einsum('rsac,rtscx->rtax', a_four, chosen, precision=lax.Precision.HI...]
    pallas_call x0 -> x2, Pallas kernels: none -> 3.53 us  [the longest x1 2.09 us: per_device(): pl.pallas_call(functools.partial(list_kernel, dims, (n_row, n_col)), out_...]
  transfers between devices with their start and end apart: 2 -> 9, of which waited for: 1 -> 5; matrix products, arithmetic and copies ran while one was open for 6% -> 0% of each run, Pallas kernels for 0% -> 6%
where the time goes in v1:
time: 35.8 us; the launch traced here: 35.6 us
  waiting for transfers between devices  16.7 us (47%)
  starting transfers between devices  14.5 us (41%)
  Pallas kernels  3.53 us (10%)
  other arithmetic  0.85 us (2%)
    ppermute x2, waiting for transfers between devices, per_device(): a_ids = [lax.ppermute(a_index.T, AXES, step) for step in a_steps]  9.83 us
    ppermute x2, waiting for transfers between devices, per_device(): b_ids = [lax.ppermute(b_index.T, AXES, step) for step in b_steps]  5.28 us
    ppermute x2, starting transfers between devices, per_device(): a_list = [rows_of(lax.ppermute(a_blocks, AXES, step)) for step in a_steps]  4.17 us
    ppermute x2, starting transfers between devices, per_device(): b_list = [rows_of(lax.ppermute(b_blocks, AXES, step)) for step in b_steps]  3.9 us
    ppermute x2, starting transfers between devices, per_device(): a_ids = [lax.ppermute(a_index.T, AXES, step) for step in a_steps]  2.77 us
    ppermute x1, starting transfers between devices, per_device(): other = lax.ppermute(part, 'depth', [(0, 1), (1, 0)])  2.16 us
    pallas_call x1, Pallas kernels, per_device(): pl.pallas_call(functools.partial(list_kernel, dims, (n_row, n_col)), out_...  2.09 us
    ppermute x1, waiting for transfers between devices, per_device(): other = lax.ppermute(part, 'depth', [(0, 1), (1, 0)])  1.54 us
  transfers between devices with their start and end apart: 9, of which 5 were waited for; matrix products, arithmetic and copies ran while one was open for 0% of the time, Pallas kernels for 6%

profile of v1, /device:TPU:0, one launch (start us, length us, event | category | flops | bytes accessed | tf_op | source)
XLA Modules:
  0.0 35.6 jit_solution(5032215994322664905)
XLA Ops:
  0.0 3.4 %collective-permute-start.7 = (f32[16,2,4096]{2,1,0:T(2,128)}, f32[16,2,4096]{2,1,0:T(2,128)S(1)}, u32[]{:S(2)}, u32[]{:S(2)}) collective-permute-start(f32[16,2,4096]{2,1,0:T(2,128)} %param.7), channel_id=1, source_target_pairs={{0,28},{1,29},{2,30},{3,31},{4,24},{5,25},{6,26},{7,27},{8,20},{9,... | collective-permute-start | bytes 1572872 | tf_op jit(solution)/shard_map/ppermute | solution.py:174
  3.4 0.5 %collective-permute-start.6 = (f32[16,2,4096]{2,1,0:T(2,128)}, f32[16,2,4096]{2,1,0:T(2,128)S(1)}, u32[]{:S(2)}, u32[]{:S(2)}) collective-permute-start(f32[16,2,4096]{2,1,0:T(2,128)} %param.7), channel_id=1, source_target_pairs={{0,4},{1,5},{2,6},{3,7},{4,0},{5,1},{6,2},{7,3},{8,12},{9,13},{10,... | collective-permute-start | bytes 1572872 | tf_op jit(solution)/shard_map/ppermute | solution.py:174
  3.9 2.6 %collective-permute-start.5 = (f32[8,2,4096]{2,1,0:T(2,128)}, f32[8,2,4096]{2,1,0:T(2,128)S(1)}, u32[]{:S(2)}, u32[]{:S(2)}) collective-permute-start(f32[8,2,4096]{2,1,0:T(2,128)} %param.5), channel_id=1, source_target_pairs={{0,2},{16,0},{18,16},{2,18},{1,3},{17,1},{19,17},{3,19},{4,6},{20,... | collective-permute-start | bytes 786440 | tf_op jit(solution)/shard_map/ppermute | solution.py:175
  6.5 1.6 %collective-permute-start.4 = (f32[8,2,4096]{2,1,0:T(2,128)}, f32[8,2,4096]{2,1,0:T(2,128)S(1)}, u32[]{:S(2)}, u32[]{:S(2)}) collective-permute-start(f32[8,2,4096]{2,1,0:T(2,128)} %param.5), channel_id=1, source_target_pairs={{16,3},{0,1},{2,17},{18,19},{17,2},{1,0},{3,16},{19,18},{20,7},{4,... | collective-permute-start | bytes 786440 | tf_op jit(solution)/shard_map/ppermute | solution.py:175
  8.1 0.0 copy-done.1
  8.1 0.0 collective-permute-start.1
  8.1 8.3 %collective-permute-done.1.refs_1_ = s32[2,8]{1,0:T(2,128)S(1)} collective-permute-done((s32[2,8]{1,0:T(2,128)S(1)}, s32[2,8]{1,0:T(2,128)S(1)}, u32[]{:S(2)}, u32[]{:S(2)}) %collective-permute-start.1) | collective-permute-done | bytes 96 | tf_op jit(solution)/shard_map/ppermute | solution.py:177
  16.4 2.8 %collective-permute-start = (s32[2,8]{1,0:T(2,128)S(1)}, s32[2,8]{1,0:T(2,128)S(1)}, u32[]{:S(2)}, u32[]{:S(2)}) collective-permute-start(s32[2,8]{1,0:T(2,128)S(1)} %bitcast.34), channel_id=1, source_target_pairs={{16,3},{0,1},{2,17},{18,19},{17,2},{1,0},{3,16},{19,18},{20,7},{4,... | collective-permute-start | bytes 200 | tf_op jit(solution)/shard_map/ppermute | solution.py:177
  19.1 1.6 %collective-permute-done.refs_0_ = s32[2,8]{1,0:T(2,128)S(1)} collective-permute-done((s32[2,8]{1,0:T(2,128)S(1)}, s32[2,8]{1,0:T(2,128)S(1)}, u32[]{:S(2)}, u32[]{:S(2)}) %collective-permute-start) | collective-permute-done | bytes 96 | tf_op jit(solution)/shard_map/ppermute | solution.py:177
  20.7 0.0 copy-done.2
  20.7 0.0 collective-permute-start.3
  20.7 3.2 %collective-permute-done.3.refs_3_ = s32[2,16]{1,0:T(2,128)S(1)} collective-permute-done((s32[2,16]{1,0:T(2,128)S(1)}, s32[2,16]{1,0:T(2,128)S(1)}, u32[]{:S(2)}, u32[]{:S(2)}) %collective-permute-start.3) | collective-permute-done | bytes 160 | tf_op jit(solution)/shard_map/ppermute | solution.py:176
  23.9 1.5 %collective-permute-start.2 = (s32[2,16]{1,0:T(2,128)S(1)}, s32[2,16]{1,0:T(2,128)S(1)}, u32[]{:S(2)}, u32[]{:S(2)}) collective-permute-start(s32[2,16]{1,0:T(2,128)S(1)} %bitcast.36), channel_id=1, source_target_pairs={{0,4},{1,5},{2,6},{3,7},{4,0},{5,1},{6,2},{7,3},{8,12},{9,13},{10,... | collective-permute-start | bytes 392 | tf_op jit(solution)/shard_map/ppermute | solution.py:176
  25.4 2.1 %collective-permute-done.2.refs_2_ = s32[2,16]{1,0:T(2,128)S(1)} collective-permute-done((s32[2,16]{1,0:T(2,128)S(1)}, s32[2,16]{1,0:T(2,128)S(1)}, u32[]{:S(2)}, u32[]{:S(2)}) %collective-permute-start.2) | collective-permute-done | bytes 160 | tf_op jit(solution)/shard_map/ppermute | solution.py:176
  27.5 0.0 copy-done
  27.5 2.1 %list.1 = (s32[1]{0:T(128)}, s32[136]{0:T(256)S(1)}, f32[1024,128]{1,0:T(8,128)S(1)}) custom-call(s32[4,8]{1,0:T(4,128)S(1)} %bitcast.32, s32[2,8]{1,0:T(2,128)S(1)} %collective-permute-done.refs_0_, s32[2,8]{1,0:T(2,128)S(1)} %collective-permute-done.1.refs_1_, s32[2,16]{1,0:T(2,128)S(1)} %collective-permute-done.2.refs_2_, ...), custom_call_target="tpu_custom_call" | custom-call | bytes 1000000 | tf_op jit(solution)/shard_map/list/pallas_call | solution.py:178
  29.6 0.0 collective-permute-done.5
  29.6 0.0 collective-permute-done.4
  29.6 0.0 collective-permute-done.7
  29.6 0.0 collective-permute-done.6
  29.6 1.4 %products.1 = f32[1024,128]{1,0:T(8,128)S(1)} custom-call(s32[1]{0:T(128)} %get-tuple-element.8.total, s32[136]{0:T(256)S(1)} %get-tuple-element.9.entries, f32[512,128]{1,0:T(8,128)S(1)} %bitcast.31, f32[512,128]{1,0:T(8,128)S(1)} %bitcast.30, f32[1024,128]{1,0:T(8,128)S(1)} %bitcast.29, f32[1024,128]{1,0:T(8,128)S(1)} %bitcast.28, ...), custom_call_target="tpu_custom_call", output_to_operand_aliasing={{}: (6, {})} | custom-call | flops 100000000 | bytes 2000000 | tf_op jit(solution)/shard_map/products/pallas_call | solution.py:187
  31.1 2.2 %collective-permute-start.8 = (f32[1024,128]{1,0:T(8,128)S(1)}, f32[1024,128]{1,0:T(8,128)S(1)}, u32[]{:S(2)}, u32[]{:S(2)}) collective-permute-start(f32[1024,128]{1,0:T(8,128)S(1)} %products.1), channel_id=1, source_target_pairs={{0,16},{16,0},{1,17},{17,1},{2,18},{18,2},{3,19},{19,3},{4,20},{20... | collective-permute-start | bytes 1572872 | tf_op jit(solution)/shard_map/ppermute | solution.py:198
  33.2 1.5 %collective-permute-done.8 = f32[1024,128]{1,0:T(8,128)S(1)} collective-permute-done((f32[1024,128]{1,0:T(8,128)S(1)}, f32[1024,128]{1,0:T(8,128)S(1)}, u32[]{:S(2)}, u32[]{:S(2)}) %collective-permute-start.8) | collective-permute-done | bytes 524320 | tf_op jit(solution)/shard_map/ppermute | solution.py:198
  34.8 0.8 %add.3 = f32[1024,128]{1,0:T(8,128)} add(f32[1024,128]{1,0:T(8,128)S(1)} %products.1, f32[1024,128]{1,0:T(8,128)S(1)} %collective-permute-done.8) | non-fusion elementwise | flops 131072 | bytes 1572864 | tf_op jit(solution)/shard_map/add | solution.py:199
  (3 shorter events, 0.0 us)
Async XLA Ops:
  0.0 8.1 %copy-start.1 = (s32[8,2]{0,1:T(2,128)S(1)}, s32[8,2]{0,1:T(2,128)}, u32[]{:S(2)}) copy-start(s32[8,2]{0,1:T(2,128)} %param.6) | copy-start | bytes 196
  0.0 29.6 %collective-permute-start.7 = (f32[16,2,4096]{2,1,0:T(2,128)}, f32[16,2,4096]{2,1,0:T(2,128)S(1)}, u32[]{:S(2)}, u32[]{:S(2)}) collective-permute-start(f32[16,2,4096]{2,1,0:T(2,128)} %param.7), channel_id=1, source_target_pairs={{0,28},{1,29},{2,30},{3,31},{4,24},{5,25},{6,26},{7,27},{8,20},{9,... | collective-permute-start | bytes 1572872 | tf_op jit(solution)/shard_map/ppermute | solution.py:174
  3.4 26.3 %collective-permute-start.6 = (f32[16,2,4096]{2,1,0:T(2,128)}, f32[16,2,4096]{2,1,0:T(2,128)S(1)}, u32[]{:S(2)}, u32[]{:S(2)}) collective-permute-start(f32[16,2,4096]{2,1,0:T(2,128)} %param.7), channel_id=1, source_target_pairs={{0,4},{1,5},{2,6},{3,7},{4,0},{5,1},{6,2},{7,3},{8,12},{9,13},{10,... | collective-permute-start | bytes 1572872 | tf_op jit(solution)/shard_map/ppermute | solution.py:174
  3.9 25.7 %collective-permute-start.5 = (f32[8,2,4096]{2,1,0:T(2,128)}, f32[8,2,4096]{2,1,0:T(2,128)S(1)}, u32[]{:S(2)}, u32[]{:S(2)}) collective-permute-start(f32[8,2,4096]{2,1,0:T(2,128)} %param.5), channel_id=1, source_target_pairs={{0,2},{16,0},{18,16},{2,18},{1,3},{17,1},{19,17},{3,19},{4,6},{20,... | collective-permute-start | bytes 786440 | tf_op jit(solution)/shard_map/ppermute | solution.py:175
  6.5 23.1 %collective-permute-start.4 = (f32[8,2,4096]{2,1,0:T(2,128)}, f32[8,2,4096]{2,1,0:T(2,128)S(1)}, u32[]{:S(2)}, u32[]{:S(2)}) collective-permute-start(f32[8,2,4096]{2,1,0:T(2,128)} %param.5), channel_id=1, source_target_pairs={{16,3},{0,1},{2,17},{18,19},{17,2},{1,0},{3,16},{19,18},{20,7},{4,... | collective-permute-start | bytes 786440 | tf_op jit(solution)/shard_map/ppermute | solution.py:175
  8.1 12.6 %copy-start.2 = (s32[16,2]{0,1:T(2,128)S(1)}, s32[16,2]{0,1:T(2,128)}, u32[]{:S(2)}) copy-start(s32[16,2]{0,1:T(2,128)} %param.8) | copy-start | bytes 388
  8.1 19.4 %copy-start = (s32[8,4]{0,1:T(4,128)S(1)}, s32[8,4]{0,1:T(4,128)}, u32[]{:S(2)}) copy-start(s32[8,4]{0,1:T(4,128)} %param.9) | copy-start | bytes 388
  8.1 8.3 %collective-permute-start.1 = (s32[2,8]{1,0:T(2,128)S(1)}, s32[2,8]{1,0:T(2,128)S(1)}, u32[]{:S(2)}, u32[]{:S(2)}) collective-permute-start(s32[2,8]{1,0:T(2,128)S(1)} %bitcast.33), channel_id=1, source_target_pairs={{0,2},{16,0},{18,16},{2,18},{1,3},{17,1},{19,17},{3,19},{4,6},{20,... | collective-permute-start | bytes 200 | tf_op jit(solution)/shard_map/ppermute | solution.py:177
  16.4 4.3 %collective-permute-start = (s32[2,8]{1,0:T(2,128)S(1)}, s32[2,8]{1,0:T(2,128)S(1)}, u32[]{:S(2)}, u32[]{:S(2)}) collective-permute-start(s32[2,8]{1,0:T(2,128)S(1)} %bitcast.34), channel_id=1, source_target_pairs={{16,3},{0,1},{2,17},{18,19},{17,2},{1,0},{3,16},{19,18},{20,7},{4,... | collective-permute-start | bytes 200 | tf_op jit(solution)/shard_map/ppermute | solution.py:177
  20.7 3.2 %collective-permute-start.3 = (s32[2,16]{1,0:T(2,128)S(1)}, s32[2,16]{1,0:T(2,128)S(1)}, u32[]{:S(2)}, u32[]{:S(2)}) collective-permute-start(s32[2,16]{1,0:T(2,128)S(1)} %bitcast.35), channel_id=1, source_target_pairs={{0,28},{1,29},{2,30},{3,31},{4,24},{5,25},{6,26},{7,27},{8,20},{9,... | collective-permute-start | bytes 392 | tf_op jit(solution)/shard_map/ppermute | solution.py:176
  23.9 3.6 %collective-permute-start.2 = (s32[2,16]{1,0:T(2,128)S(1)}, s32[2,16]{1,0:T(2,128)S(1)}, u32[]{:S(2)}, u32[]{:S(2)}) collective-permute-start(s32[2,16]{1,0:T(2,128)S(1)} %bitcast.36), channel_id=1, source_target_pairs={{0,4},{1,5},{2,6},{3,7},{4,0},{5,1},{6,2},{7,3},{8,12},{9,13},{10,... | collective-permute-start | bytes 392 | tf_op jit(solution)/shard_map/ppermute | solution.py:176
  31.1 3.7 %collective-permute-start.8 = (f32[1024,128]{1,0:T(8,128)S(1)}, f32[1024,128]{1,0:T(8,128)S(1)}, u32[]{:S(2)}, u32[]{:S(2)}) collective-permute-start(f32[1024,128]{1,0:T(8,128)S(1)} %products.1), channel_id=1, source_target_pairs={{0,16},{16,0},{1,17},{17,1},{2,18},{18,2},{3,19},{19,3},{4,20},{20... | collective-permute-start | bytes 1572872 | tf_op jit(solution)/shard_map/ppermute | solution.py:198

commit v2 on v1

--- a/solution.py
+++ b/solution.py
@@ -29,6 +29,11 @@
     b_steps.append(
         [((0, i, j), (1, i ^ (n_row - 1), j)) for i, j in chips] + [((1, i, j), (0, i, j)) for i, j in chips]
     )
+    b_marks = [
+        [((1 - d, i, j), (d, i ^ hop, j)) for d, hop in enumerate((k, half + k - 1)) for i, j in chips]
+        for k in range(1, half)
+    ]
+    b_marks.append([((d, i, j), (d, i ^ hop, j)) for d, hop in enumerate((half, n_row - 1)) for i, j in chips])
     a_steps = []
     for r in reversed(range(n)):
         step = []
@@ -47,9 +52,9 @@
                         step.append(((1 - d, i, here), (d, i, here)))
         a_steps.append(step)
     flat = lambda steps: [[(place(*s), place(*t)) for s, t in step] for step in steps]
-    for step in flat(a_steps) + flat(b_steps):
+    for step in flat(a_steps) + flat(b_steps) + flat(b_marks):
         assert [sorted(x) for x in zip(*step)] == [list(range(2 * n_row * n_col))] * 2
-    return flat(a_steps), flat(b_steps)
+    return flat(a_steps), flat(b_steps), flat(b_marks)
 
 
 def rows_of(blocks):
@@ -90,11 +95,11 @@
     n_row, n_col = mesh_dims
     n_a, n_b, ratio = n_col // 2, n_row // 2, n_col // n_row
     a_ids, b_ids = refs[:n_a], refs[n_a : n_a + n_b]
-    total, entries, out = refs[n_a + n_b :]
+    own, entries, out = refs[n_a + n_b :]
     sizes = (rows, sc, cols, n_a, sa, n_b, sb)
     core, i, j = (lax.axis_index(name) for name in AXES)
     out[...] = jnp.zeros_like(out)
-    count = jnp.int32(0)
+    count = jnp.int32(1)
     for x in range(n_b):
         q = i ^ jnp.where(core == 0, (x + 1) % n_b, n_b + x)
         for r in range(ratio):
@@ -110,7 +115,10 @@
                     n = c_ids[t, m]
                     at = jnp.maximum(n, 0)
                     for u in range(sb):
-                        k = jnp.where(n < 0, -1, b_ids[x][u, at])
+                        k = b_ids[x][u, at]
+                        if x == n_b - 1:
+                            k = jnp.where(core == 0, own[u, at], k)
+                        k = jnp.where(n < 0, -1, k)
                         slot, hit = jnp.int32(0), k == mine[0]
                         for s in range(1, sa):
                             slot = jnp.where(k == mine[s], s, slot)
@@ -119,19 +127,19 @@
                         count = count + hit.astype(jnp.int32)
     for k in range(UNROLL):
         entries[count + k] = 0
-    total[0] = count
-
-
-def product_kernel(dims, n_a, n_b, total, entries, *refs):
+    entries[0] = count - 1
+
+
+def product_kernel(dims, n_a, n_b, entries, *refs):
     rows, cols, sa, sb, sc = dims
     a_refs, b_refs = refs[:n_a], refs[n_a : n_a + n_b]
     _, out, spread = refs[n_a + n_b :]
     sizes = (rows, sc, cols, n_a, sa, n_b, sb)
-    count = total[0]
+    count = entries[0]
     low = lax.broadcasted_iota(jnp.int32, (HALF, LANES), 1) < BS
 
     def one(e, lane):
-        m, t, c, a, s, b, u = unpacked(entries[e], sizes)
+        m, t, c, a, s, b, u = unpacked(entries[1 + e], sizes)
         x = pick(a_refs, a, m * (sa * HALF) + s, sa)
         x = jnp.where(e < count, x, 0.0)
         y = pick(b_refs, b, c * (sb * HALF) + u, sb)
@@ -165,7 +173,7 @@
 
 
 def per_device(n_row, n_col, a_blocks, a_index, b_blocks, b_index, c_index):
-    a_steps, b_steps = plan(n_row, n_col)
+    a_steps, b_steps, b_marks = plan(n_row, n_col)
     dims = (a_index.shape[0], b_index.shape[0], a_index.shape[1], b_index.shape[1], c_index.shape[1])
     rows, _, sa, _, sc = dims
     full = jax.ShapeDtypeStruct((rows * HALF * sc, LANES), jnp.float32)
@@ -173,28 +181,28 @@
 
     b_list = [rows_of(lax.ppermute(b_blocks, AXES, step)) for step in b_steps]
     a_list = [rows_of(lax.ppermute(a_blocks, AXES, step)) for step in a_steps]
-    b_ids = [lax.ppermute(b_index.T, AXES, step) for step in b_steps]
+    b_ids = [lax.ppermute(b_index.T, AXES, step) for step in b_marks]
     a_ids = [lax.ppermute(a_index.T, AXES, step) for step in a_steps]
-    count, entries, empty = pl.pallas_call(
+    entries, empty = pl.pallas_call(
         functools.partial(list_kernel, dims, (n_row, n_col)),
-        out_shape=[jax.ShapeDtypeStruct((1,), jnp.int32), jax.ShapeDtypeStruct((cap,), jnp.int32), full],
-        in_specs=[SMEM] * (1 + len(a_ids) + len(b_ids)),
-        out_specs=[SMEM, SMEM, VMEM],
+        out_shape=[jax.ShapeDtypeStruct((cap,), jnp.int32), full],
+        in_specs=[SMEM] * (2 + len(a_ids) + len(b_ids)),
+        out_specs=[SMEM, VMEM],
         compiler_params=pltpu.CompilerParams(vmem_limit_bytes=16 * 1024 * 1024),
         cost_estimate=pl.CostEstimate(flops=0, bytes_accessed=1_000_000, transcendentals=0),
         name="list",
-    )(c_index.T, *a_ids, *b_ids)
+    )(c_index.T, *a_ids, *b_ids, b_index.T)
     part = pl.pallas_call(
         functools.partial(product_kernel, dims, len(a_list), len(b_list)),
         out_shape=full,
-        in_specs=[SMEM] * 2 + [VMEM] * (len(a_list) + len(b_list) + 1),
+        in_specs=[SMEM] + [VMEM] * (len(a_list) + len(b_list) + 1),
         out_specs=VMEM,
         scratch_shapes=[pltpu.VMEM((UNROLL, LANES, LANES), jnp.float32)],
-        input_output_aliases={2 + len(a_list) + len(b_list): 0},
+        input_output_aliases={1 + len(a_list) + len(b_list): 0},
         compiler_params=pltpu.CompilerParams(vmem_limit_bytes=16 * 1024 * 1024),
         cost_estimate=pl.CostEstimate(flops=100_000_000, bytes_accessed=2_000_000, transcendentals=0),
         name="products",
-    )(count, entries, *a_list, *b_list, empty)
+    )(entries, *a_list, *b_list, empty)
     other = lax.ppermute(part, "depth", [(0, 1), (1, 0)])
     return blocks_of(part + other, rows, sc)
 

time: 35.8 us -> 35.5 us (level)
  starting transfers between devices: 14.5 us -> 15.6 us
  waiting for transfers between devices: 16.7 us -> 15.8 us
  Pallas kernels: 3.53 us -> 3 us
    ppermute x2, starting transfers between devices: 1.53 us -> 4.27 us  [per_device(): b_ids = [lax.ppermute(b_index.T, AXES, step) for step in b_marks]]
    ppermute x1, starting transfers between devices: 2.16 us -> 0.46 us  [per_device(): other = lax.ppermute(part, 'depth', [(0, 1), (1, 0)])]
    ppermute x2, waiting for transfers between devices: 5.28 us -> 4.46 us  [per_device(): b_ids = [lax.ppermute(b_index.T, AXES, step) for step in b_marks]]
    pallas_call x1, Pallas kernels: 1.45 us -> 0.8 us  [per_device(): pl.pallas_call(functools.partial(product_kernel, dims, len(a_list), len(b...]
where the time goes in v2:
time: 35.5 us; the launch traced here: 35.3 us
  waiting for transfers between devices  15.8 us (45%)
  starting transfers between devices  15.6 us (44%)
  Pallas kernels  3 us (8%)
  other arithmetic  0.85 us (2%)
    ppermute x2, waiting for transfers between devices, per_device(): a_ids = [lax.ppermute(a_index.T, AXES, step) for step in a_steps]  9.83 us
    ppermute x2, waiting for transfers between devices, per_device(): b_ids = [lax.ppermute(b_index.T, AXES, step) for step in b_marks]  4.46 us
    ppermute x2, starting transfers between devices, per_device(): b_ids = [lax.ppermute(b_index.T, AXES, step) for step in b_marks]  4.27 us
    ppermute x2, starting transfers between devices, per_device(): a_list = [rows_of(lax.ppermute(a_blocks, AXES, step)) for step in a_steps]  4.17 us
    ppermute x2, starting transfers between devices, per_device(): b_list = [rows_of(lax.ppermute(b_blocks, AXES, step)) for step in b_steps]  3.9 us
    ppermute x2, starting transfers between devices, per_device(): a_ids = [lax.ppermute(a_index.T, AXES, step) for step in a_steps]  2.77 us
    pallas_call x1, Pallas kernels, per_device(): pl.pallas_call(functools.partial(list_kernel, dims, (n_row, n_col)), out_...  2.19 us
    ppermute x1, waiting for transfers between devices, per_device(): other = lax.ppermute(part, 'depth', [(0, 1), (1, 0)])  1.54 us
  transfers between devices with their start and end apart: 9, of which 5 were waited for; matrix products, arithmetic and copies ran while one was open for 0% of the time, Pallas kernels for 6%

profile of v2, /device:TPU:0, one launch (start us, length us, event | category | flops | bytes accessed | tf_op | source)
XLA Modules:
  0.0 35.3 jit_solution(16122917332835971971)
XLA Ops:
  0.0 3.4 %collective-permute-start.7 = (f32[16,2,4096]{2,1,0:T(2,128)}, f32[16,2,4096]{2,1,0:T(2,128)S(1)}, u32[]{:S(2)}, u32[]{:S(2)}) collective-permute-start(f32[16,2,4096]{2,1,0:T(2,128)} %param.7), channel_id=1, source_target_pairs={{0,28},{1,29},{2,30},{3,31},{4,24},{5,25},{6,26},{7,27},{8,20},{9,... | collective-permute-start | bytes 1572872 | tf_op jit(solution)/shard_map/ppermute | solution.py:182
  3.4 0.5 %collective-permute-start.6 = (f32[16,2,4096]{2,1,0:T(2,128)}, f32[16,2,4096]{2,1,0:T(2,128)S(1)}, u32[]{:S(2)}, u32[]{:S(2)}) collective-permute-start(f32[16,2,4096]{2,1,0:T(2,128)} %param.7), channel_id=1, source_target_pairs={{0,4},{1,5},{2,6},{3,7},{4,0},{5,1},{6,2},{7,3},{8,12},{9,13},{10,... | collective-permute-start | bytes 1572872 | tf_op jit(solution)/shard_map/ppermute | solution.py:182
  3.9 2.6 %collective-permute-start.5 = (f32[8,2,4096]{2,1,0:T(2,128)}, f32[8,2,4096]{2,1,0:T(2,128)S(1)}, u32[]{:S(2)}, u32[]{:S(2)}) collective-permute-start(f32[8,2,4096]{2,1,0:T(2,128)} %param.5), channel_id=1, source_target_pairs={{0,2},{16,0},{18,16},{2,18},{1,3},{17,1},{19,17},{3,19},{4,6},{20,... | collective-permute-start | bytes 786440 | tf_op jit(solution)/shard_map/ppermute | solution.py:183
  6.5 1.6 %collective-permute-start.4 = (f32[8,2,4096]{2,1,0:T(2,128)}, f32[8,2,4096]{2,1,0:T(2,128)S(1)}, u32[]{:S(2)}, u32[]{:S(2)}) collective-permute-start(f32[8,2,4096]{2,1,0:T(2,128)} %param.5), channel_id=1, source_target_pairs={{16,3},{0,1},{2,17},{18,19},{17,2},{1,0},{3,16},{19,18},{20,7},{4,... | collective-permute-start | bytes 786440 | tf_op jit(solution)/shard_map/ppermute | solution.py:183
  8.1 0.0 copy-done.2
  8.1 0.0 collective-permute-start.1
  8.1 8.3 %collective-permute-done.1.refs_1_ = s32[2,8]{1,0:T(2,128)S(1)} collective-permute-done((s32[2,8]{1,0:T(2,128)S(1)}, s32[2,8]{1,0:T(2,128)S(1)}, u32[]{:S(2)}, u32[]{:S(2)}) %collective-permute-start.1) | collective-permute-done | bytes 96 | tf_op jit(solution)/shard_map/ppermute | solution.py:185
  16.4 2.8 %collective-permute-start = (s32[2,8]{1,0:T(2,128)S(1)}, s32[2,8]{1,0:T(2,128)S(1)}, u32[]{:S(2)}, u32[]{:S(2)}) collective-permute-start(s32[2,8]{1,0:T(2,128)S(1)} %bitcast.37), channel_id=1, source_target_pairs={{16,3},{0,1},{2,17},{18,19},{17,2},{1,0},{3,16},{19,18},{20,7},{4,... | collective-permute-start | bytes 200 | tf_op jit(solution)/shard_map/ppermute | solution.py:185
  19.1 1.6 %collective-permute-done.refs_0_ = s32[2,8]{1,0:T(2,128)S(1)} collective-permute-done((s32[2,8]{1,0:T(2,128)S(1)}, s32[2,8]{1,0:T(2,128)S(1)}, u32[]{:S(2)}, u32[]{:S(2)}) %collective-permute-start) | collective-permute-done | bytes 96 | tf_op jit(solution)/shard_map/ppermute | solution.py:185
  20.7 0.0 copy-done.1
  20.7 4.2 %collective-permute-start.3 = (s32[2,16]{1,0:T(2,128)S(1)}, s32[2,16]{1,0:T(2,128)S(1)}, u32[]{:S(2)}, u32[]{:S(2)}) collective-permute-start(s32[2,16]{1,0:T(2,128)S(1)} %bitcast.33), channel_id=1, source_target_pairs={{0,8},{1,9},{2,10},{3,11},{4,12},{5,13},{6,14},{7,15},{8,0},{9,1},... | collective-permute-start | bytes 392 | tf_op jit(solution)/shard_map/ppermute | solution.py:184
  24.9 1.6 %collective-permute-done.3.refs_3_ = s32[2,16]{1,0:T(2,128)S(1)} collective-permute-done((s32[2,16]{1,0:T(2,128)S(1)}, s32[2,16]{1,0:T(2,128)S(1)}, u32[]{:S(2)}, u32[]{:S(2)}) %collective-permute-start.3) | collective-permute-done | bytes 160 | tf_op jit(solution)/shard_map/ppermute | solution.py:184
  26.4 0.1 collective-permute-start.2
  26.5 2.9 %collective-permute-done.2.refs_2_ = s32[2,16]{1,0:T(2,128)S(1)} collective-permute-done((s32[2,16]{1,0:T(2,128)S(1)}, s32[2,16]{1,0:T(2,128)S(1)}, u32[]{:S(2)}, u32[]{:S(2)}) %collective-permute-start.2) | collective-permute-done | bytes 160 | tf_op jit(solution)/shard_map/ppermute | solution.py:184
  29.4 0.0 copy-done
  29.4 2.2 %list.1 = (s32[136]{0:T(256)S(1)}, f32[1024,128]{1,0:T(8,128)S(1)}) custom-call(s32[4,8]{1,0:T(4,128)S(1)} %bitcast.32, s32[2,8]{1,0:T(2,128)S(1)} %collective-permute-done.refs_0_, s32[2,8]{1,0:T(2,128)S(1)} %collective-permute-done.1.refs_1_, s32[2,16]{1,0:T(2,128)S(1)} %collective-permute-done.2.refs_2_, s32[2,16]{1,0:T(2,128)S(1)} %collective-permute-done.3.refs_3_, ...), custom_call_target="tpu_custom_call" | custom-call | bytes 1000000 | tf_op jit(solution)/shard_map/list/pallas_call | solution.py:186
  31.6 0.0 collective-permute-done.5
  31.6 0.0 collective-permute-done.4
  31.6 0.0 collective-permute-done.7
  31.7 0.0 collective-permute-done.6
  31.7 0.8 %products.1 = f32[1024,128]{1,0:T(8,128)S(1)} custom-call(s32[136]{0:T(256)S(1)} %get-tuple-element.7.entries, f32[512,128]{1,0:T(8,128)S(1)} %bitcast.31, f32[512,128]{1,0:T(8,128)S(1)} %bitcast.30, f32[1024,128]{1,0:T(8,128)S(1)} %bitcast.29, f32[1024,128]{1,0:T(8,128)S(1)} %bitcast.28, ...), custom_call_target="tpu_custom_call", output_to_operand_aliasing={{}: (5, {})} | custom-call | flops 100000000 | bytes 2000000 | tf_op jit(solution)/shard_map/products/pallas_call | solution.py:195
  32.5 0.5 %collective-permute-start.8 = (f32[1024,128]{1,0:T(8,128)S(1)}, f32[1024,128]{1,0:T(8,128)S(1)}, u32[]{:S(2)}, u32[]{:S(2)}) collective-permute-start(f32[1024,128]{1,0:T(8,128)S(1)} %products.1), channel_id=1, source_target_pairs={{0,16},{16,0},{1,17},{17,1},{2,18},{18,2},{3,19},{19,3},{4,20},{20... | collective-permute-start | bytes 1572872 | tf_op jit(solution)/shard_map/ppermute | solution.py:206
  32.9 1.5 %collective-permute-done.8 = f32[1024,128]{1,0:T(8,128)S(1)} collective-permute-done((f32[1024,128]{1,0:T(8,128)S(1)}, f32[1024,128]{1,0:T(8,128)S(1)}, u32[]{:S(2)}, u32[]{:S(2)}) %collective-permute-start.8) | collective-permute-done | bytes 524320 | tf_op jit(solution)/shard_map/ppermute | solution.py:206
  34.5 0.8 %add.3 = f32[1024,128]{1,0:T(8,128)} add(f32[1024,128]{1,0:T(8,128)S(1)} %products.1, f32[1024,128]{1,0:T(8,128)S(1)} %collective-permute-done.8) | non-fusion elementwise | flops 131072 | bytes 1572864 | tf_op jit(solution)/shard_map/add | solution.py:207
  (3 shorter events, 0.0 us)
Async XLA Ops:
  0.0 8.1 %copy-start.2 = (s32[8,2]{0,1:T(2,128)S(1)}, s32[8,2]{0,1:T(2,128)}, u32[]{:S(2)}) copy-start(s32[8,2]{0,1:T(2,128)} %param.6) | copy-start | bytes 196
  0.0 31.6 %collective-permute-start.7 = (f32[16,2,4096]{2,1,0:T(2,128)}, f32[16,2,4096]{2,1,0:T(2,128)S(1)}, u32[]{:S(2)}, u32[]{:S(2)}) collective-permute-start(f32[16,2,4096]{2,1,0:T(2,128)} %param.7), channel_id=1, source_target_pairs={{0,28},{1,29},{2,30},{3,31},{4,24},{5,25},{6,26},{7,27},{8,20},{9,... | collective-permute-start | bytes 1572872 | tf_op jit(solution)/shard_map/ppermute | solution.py:182
  3.4 28.3 %collective-permute-start.6 = (f32[16,2,4096]{2,1,0:T(2,128)}, f32[16,2,4096]{2,1,0:T(2,128)S(1)}, u32[]{:S(2)}, u32[]{:S(2)}) collective-permute-start(f32[16,2,4096]{2,1,0:T(2,128)} %param.7), channel_id=1, source_target_pairs={{0,4},{1,5},{2,6},{3,7},{4,0},{5,1},{6,2},{7,3},{8,12},{9,13},{10,... | collective-permute-start | bytes 1572872 | tf_op jit(solution)/shard_map/ppermute | solution.py:182
  3.9 27.7 %collective-permute-start.5 = (f32[8,2,4096]{2,1,0:T(2,128)}, f32[8,2,4096]{2,1,0:T(2,128)S(1)}, u32[]{:S(2)}, u32[]{:S(2)}) collective-permute-start(f32[8,2,4096]{2,1,0:T(2,128)} %param.5), channel_id=1, source_target_pairs={{0,2},{16,0},{18,16},{2,18},{1,3},{17,1},{19,17},{3,19},{4,6},{20,... | collective-permute-start | bytes 786440 | tf_op jit(solution)/shard_map/ppermute | solution.py:183
  6.5 25.1 %collective-permute-start.4 = (f32[8,2,4096]{2,1,0:T(2,128)}, f32[8,2,4096]{2,1,0:T(2,128)S(1)}, u32[]{:S(2)}, u32[]{:S(2)}) collective-permute-start(f32[8,2,4096]{2,1,0:T(2,128)} %param.5), channel_id=1, source_target_pairs={{16,3},{0,1},{2,17},{18,19},{17,2},{1,0},{3,16},{19,18},{20,7},{4,... | collective-permute-start | bytes 786440 | tf_op jit(solution)/shard_map/ppermute | solution.py:183
  8.1 12.6 %copy-start.1 = (s32[16,2]{0,1:T(2,128)S(1)}, s32[16,2]{0,1:T(2,128)}, u32[]{:S(2)}) copy-start(s32[16,2]{0,1:T(2,128)} %param.8) | copy-start | bytes 388
  8.1 21.4 %copy-start = (s32[8,4]{0,1:T(4,128)S(1)}, s32[8,4]{0,1:T(4,128)}, u32[]{:S(2)}) copy-start(s32[8,4]{0,1:T(4,128)} %param.9) | copy-start | bytes 388
  8.1 8.3 %collective-permute-start.1 = (s32[2,8]{1,0:T(2,128)S(1)}, s32[2,8]{1,0:T(2,128)S(1)}, u32[]{:S(2)}, u32[]{:S(2)}) collective-permute-start(s32[2,8]{1,0:T(2,128)S(1)} %bitcast.36), channel_id=1, source_target_pairs={{0,2},{16,0},{18,16},{2,18},{1,3},{17,1},{19,17},{3,19},{4,6},{20,... | collective-permute-start | bytes 200 | tf_op jit(solution)/shard_map/ppermute | solution.py:185
  16.4 4.3 %collective-permute-start = (s32[2,8]{1,0:T(2,128)S(1)}, s32[2,8]{1,0:T(2,128)S(1)}, u32[]{:S(2)}, u32[]{:S(2)}) collective-permute-start(s32[2,8]{1,0:T(2,128)S(1)} %bitcast.37), channel_id=1, source_target_pairs={{16,3},{0,1},{2,17},{18,19},{17,2},{1,0},{3,16},{19,18},{20,7},{4,... | collective-permute-start | bytes 200 | tf_op jit(solution)/shard_map/ppermute | solution.py:185
  20.7 5.7 %collective-permute-start.3 = (s32[2,16]{1,0:T(2,128)S(1)}, s32[2,16]{1,0:T(2,128)S(1)}, u32[]{:S(2)}, u32[]{:S(2)}) collective-permute-start(s32[2,16]{1,0:T(2,128)S(1)} %bitcast.33), channel_id=1, source_target_pairs={{0,8},{1,9},{2,10},{3,11},{4,12},{5,13},{6,14},{7,15},{8,0},{9,1},... | collective-permute-start | bytes 392 | tf_op jit(solution)/shard_map/ppermute | solution.py:184
  26.4 3.0 %collective-permute-start.2 = (s32[2,16]{1,0:T(2,128)S(1)}, s32[2,16]{1,0:T(2,128)S(1)}, u32[]{:S(2)}, u32[]{:S(2)}) collective-permute-start(s32[2,16]{1,0:T(2,128)S(1)} %bitcast.34), channel_id=1, source_target_pairs={{16,4},{17,5},{18,6},{19,7},{20,0},{21,1},{22,2},{23,3},{24,12},{2... | collective-permute-start | bytes 392 | tf_op jit(solution)/shard_map/ppermute | solution.py:184
  32.5 2.0 %collective-permute-start.8 = (f32[1024,128]{1,0:T(8,128)S(1)}, f32[1024,128]{1,0:T(8,128)S(1)}, u32[]{:S(2)}, u32[]{:S(2)}) collective-permute-start(f32[1024,128]{1,0:T(8,128)S(1)} %products.1), channel_id=1, source_target_pairs={{0,16},{16,0},{1,17},{17,1},{2,18},{18,2},{3,19},{19,3},{4,20},{20... | collective-permute-start | bytes 1572872 | tf_op jit(solution)/shard_map/ppermute | solution.py:206

commit v3 on v2

--- a/solution.py
+++ b/solution.py
@@ -12,7 +12,7 @@
 LANES = 128
 HALF = BS * BS // LANES
 AXES = ("depth", "row", "col")
-UNROLL = 2
+UNROLL = 4
 VMEM = pl.BlockSpec(memory_space=pltpu.VMEM)
 SMEM = pl.BlockSpec(memory_space=pltpu.SMEM)
 
@@ -35,7 +35,7 @@
     ]
     b_marks.append([((d, i, j), (d, i ^ hop, j)) for d, hop in enumerate((half, n_row - 1)) for i, j in chips])
     a_steps = []
-    for r in reversed(range(n)):
+    for r in range(n):
         step = []
         for i in range(n_row):
             kinds = [[], []]
@@ -44,9 +44,9 @@
             for q in range(n):
                 for d in (0, 1):
                     here, there = kinds[d][q], kinds[1 - d][q ^ r]
-                    if r:
+                    if r < n - 1:
                         step.append(((1 - d, i, here), (d, i, there)))
-                        step.append(((d, i, here), (d, i, kinds[d][q ^ r])))
+                        step.append(((d, i, here), (d, i, kinds[d][q ^ (r + 1)])))
                     else:
                         step.append(((d, i, here), (d, i, there)))
                         step.append(((1 - d, i, here), (d, i, here)))
@@ -99,32 +99,41 @@
     sizes = (rows, sc, cols, n_a, sa, n_b, sb)
     core, i, j = (lax.axis_index(name) for name in AXES)
     out[...] = jnp.zeros_like(out)
-    count = jnp.int32(1)
+    panels = []
     for x in range(n_b):
         q = i ^ jnp.where(core == 0, (x + 1) % n_b, n_b + x)
         for r in range(ratio):
-            which = n_a - 1 - (((q * ratio + r) ^ j) & (n_a - 1))
-            for m in range(rows):
-                mine = []
-                for s in range(sa):
-                    k = a_ids[0][s, m]
-                    for a in range(1, n_a):
-                        k = jnp.where(which == a, a_ids[a][s, m], k)
-                    mine.append(jnp.where(k < 0, -2, k))
-                for t in range(sc):
-                    n = c_ids[t, m]
-                    at = jnp.maximum(n, 0)
-                    for u in range(sb):
-                        k = b_ids[x][u, at]
-                        if x == n_b - 1:
-                            k = jnp.where(core == 0, own[u, at], k)
-                        k = jnp.where(n < 0, -1, k)
-                        slot, hit = jnp.int32(0), k == mine[0]
-                        for s in range(1, sa):
-                            slot = jnp.where(k == mine[s], s, slot)
-                            hit = hit | (k == mine[s])
-                        entries[count] = packed(list(zip((m, t, at, which, slot, x, u), sizes)))
-                        count = count + hit.astype(jnp.int32)
+            apart = (q * ratio + r) ^ j
+            which = jnp.where(apart & n_a != 0, apart, apart - 1) & (n_a - 1)
+            panels.append((x, which, packed(list(zip((0, 0, 0, which, 0, x, 0), sizes)))))
+    second = [packed(list(zip((0, 0, 0, 0, s, 0, 0), sizes))) for s in range(sa)]
+    count = jnp.int32(1)
+    for m in range(rows):
+        mine = []
+        for _, which, _ in panels:
+            ks = []
+            for s in range(sa):
+                k = a_ids[0][s, m]
+                for a in range(1, n_a):
+                    k = jnp.where(which == a, a_ids[a][s, m], k)
+                ks.append(jnp.where(k < 0, -2, k))
+            mine.append(ks)
+        for t in range(sc):
+            n = c_ids[t, m]
+            at = jnp.maximum(n, 0)
+            base = packed(list(zip((m, t, at, 0, 0, 0, 0), sizes)))
+            for (x, _, code), ks in zip(panels, mine):
+                for u in range(sb):
+                    k = b_ids[x][u, at]
+                    if x == n_b - 1:
+                        k = jnp.where(core == 0, own[u, at], k)
+                    k = jnp.where(n < 0, -1, k)
+                    slot, hit = jnp.int32(0), k == ks[0]
+                    for s in range(1, sa):
+                        slot = jnp.where(k == ks[s], second[s], slot)
+                        hit = hit | (k == ks[s])
+                    entries[count] = base + code + (slot + u)
+                    count = count + hit.astype(jnp.int32)
     for k in range(UNROLL):
         entries[count + k] = 0
     entries[0] = count - 1

time: 35.5 us -> 34.4 us (0.969)
  starting transfers between devices: 15.6 us -> 14.8 us
    ppermute x2, starting transfers between devices: 4.27 us -> 2.65 us  [per_device(): b_ids = [lax.ppermute(b_index.T, AXES, step) for step in b_marks]]
    ppermute x2, starting transfers between devices: 2.77 us -> 3.93 us  [per_device(): a_ids = [lax.ppermute(a_index.T, AXES, step) for step in a_steps]]
    ppermute x2, starting transfers between devices: 4.17 us -> 3.6 us  [per_device(): a_list = [rows_of(lax.ppermute(a_blocks, AXES, step)) for step in a_steps]]
    ppermute x2, waiting for transfers between devices: 9.83 us -> 9.38 us  [per_device(): a_ids = [lax.ppermute(a_index.T, AXES, step) for step in a_steps]]
where the time goes in v3:
time: 34.4 us; the launch traced here: 34.2 us
  waiting for transfers between devices  15.6 us (45%)
  starting transfers between devices  14.8 us (43%)
  Pallas kernels  2.86 us (8%)
  other arithmetic  0.85 us (2%)
    ppermute x2, waiting for transfers between devices, per_device(): a_ids = [lax.ppermute(a_index.T, AXES, step) for step in a_steps]  9.38 us
    ppermute x2, waiting for transfers between devices, per_device(): b_ids = [lax.ppermute(b_index.T, AXES, step) for step in b_marks]  4.72 us
    ppermute x2, starting transfers between devices, per_device(): a_ids = [lax.ppermute(a_index.T, AXES, step) for step in a_steps]  3.93 us
    ppermute x2, starting transfers between devices, per_device(): b_list = [rows_of(lax.ppermute(b_blocks, AXES, step)) for step in b_steps]  3.9 us
    ppermute x2, starting transfers between devices, per_device(): a_list = [rows_of(lax.ppermute(a_blocks, AXES, step)) for step in a_steps]  3.6 us
    ppermute x2, starting transfers between devices, per_device(): b_ids = [lax.ppermute(b_index.T, AXES, step) for step in b_marks]  2.65 us
    pallas_call x1, Pallas kernels, per_device(): pl.pallas_call(functools.partial(list_kernel, dims, (n_row, n_col)), out_...  2.02 us
    ppermute x1, waiting for transfers between devices, per_device(): other = lax.ppermute(part, 'depth', [(0, 1), (1, 0)])  1.54 us
  transfers between devices with their start and end apart: 9, of which 5 were waited for; matrix products, arithmetic and copies ran while one was open for 0% of the time, Pallas kernels for 6%

profile of v3, /device:TPU:0, one launch (start us, length us, event | category | flops | bytes accessed | tf_op | source)
XLA Modules:
  0.0 34.2 jit_solution(14771028216913854379)
XLA Ops:
  0.0 3.4 %collective-permute-start.7 = (f32[16,2,4096]{2,1,0:T(2,128)}, f32[16,2,4096]{2,1,0:T(2,128)S(1)}, u32[]{:S(2)}, u32[]{:S(2)}) collective-permute-start(f32[16,2,4096]{2,1,0:T(2,128)} %param.7), channel_id=1, source_target_pairs={{0,28},{1,29},{2,30},{3,31},{4,24},{5,25},{6,26},{7,27},{8,20},{9,... | collective-permute-start | bytes 1572872 | tf_op jit(solution)/shard_map/ppermute | solution.py:191
  3.4 0.5 %collective-permute-start.6 = (f32[16,2,4096]{2,1,0:T(2,128)}, f32[16,2,4096]{2,1,0:T(2,128)S(1)}, u32[]{:S(2)}, u32[]{:S(2)}) collective-permute-start(f32[16,2,4096]{2,1,0:T(2,128)} %param.7), channel_id=1, source_target_pairs={{0,4},{1,5},{2,6},{3,7},{4,0},{5,1},{6,2},{7,3},{8,12},{9,13},{10,... | collective-permute-start | bytes 1572872 | tf_op jit(solution)/shard_map/ppermute | solution.py:191
  3.9 3.6 %collective-permute-start.5 = (f32[8,2,4096]{2,1,0:T(2,128)}, f32[8,2,4096]{2,1,0:T(2,128)S(1)}, u32[]{:S(2)}, u32[]{:S(2)}) collective-permute-start(f32[8,2,4096]{2,1,0:T(2,128)} %param.5), channel_id=1, source_target_pairs={{0,3},{16,0},{18,17},{2,18},{1,2},{17,1},{19,16},{3,19},{4,7},{20,... | collective-permute-start | bytes 786440 | tf_op jit(solution)/shard_map/ppermute | solution.py:192
  7.5 0.0 collective-permute-start.4
  7.5 0.0 copy-done.2
  7.5 0.4 %collective-permute-start.1 = (s32[2,8]{1,0:T(2,128)S(1)}, s32[2,8]{1,0:T(2,128)S(1)}, u32[]{:S(2)}, u32[]{:S(2)}) collective-permute-start(s32[2,8]{1,0:T(2,128)S(1)} %bitcast.36), channel_id=1, source_target_pairs={{0,3},{16,0},{18,17},{2,18},{1,2},{17,1},{19,16},{3,19},{4,7},{20,... | collective-permute-start | bytes 200 | tf_op jit(solution)/shard_map/ppermute | solution.py:194
  8.0 7.8 %collective-permute-done.1.refs_1_ = s32[2,8]{1,0:T(2,128)S(1)} collective-permute-done((s32[2,8]{1,0:T(2,128)S(1)}, s32[2,8]{1,0:T(2,128)S(1)}, u32[]{:S(2)}, u32[]{:S(2)}) %collective-permute-start.1) | collective-permute-done | bytes 96 | tf_op jit(solution)/shard_map/ppermute | solution.py:194
  15.8 3.5 %collective-permute-start = (s32[2,8]{1,0:T(2,128)S(1)}, s32[2,8]{1,0:T(2,128)S(1)}, u32[]{:S(2)}, u32[]{:S(2)}) collective-permute-start(s32[2,8]{1,0:T(2,128)S(1)} %bitcast.37), channel_id=1, source_target_pairs={{16,2},{0,1},{2,16},{18,19},{17,3},{1,0},{3,17},{19,18},{20,6},{4,... | collective-permute-start | bytes 200 | tf_op jit(solution)/shard_map/ppermute | solution.py:194
  19.3 1.6 %collective-permute-done.refs_0_ = s32[2,8]{1,0:T(2,128)S(1)} collective-permute-done((s32[2,8]{1,0:T(2,128)S(1)}, s32[2,8]{1,0:T(2,128)S(1)}, u32[]{:S(2)}, u32[]{:S(2)}) %collective-permute-start) | collective-permute-done | bytes 96 | tf_op jit(solution)/shard_map/ppermute | solution.py:194
  20.8 0.0 copy-done.1
  20.8 1.3 %collective-permute-start.3 = (s32[2,16]{1,0:T(2,128)S(1)}, s32[2,16]{1,0:T(2,128)S(1)}, u32[]{:S(2)}, u32[]{:S(2)}) collective-permute-start(s32[2,16]{1,0:T(2,128)S(1)} %bitcast.33), channel_id=1, source_target_pairs={{0,8},{1,9},{2,10},{3,11},{4,12},{5,13},{6,14},{7,15},{8,0},{9,1},... | collective-permute-start | bytes 392 | tf_op jit(solution)/shard_map/ppermute | solution.py:193
  22.1 2.3 %collective-permute-done.3.refs_3_ = s32[2,16]{1,0:T(2,128)S(1)} collective-permute-done((s32[2,16]{1,0:T(2,128)S(1)}, s32[2,16]{1,0:T(2,128)S(1)}, u32[]{:S(2)}, u32[]{:S(2)}) %collective-permute-start.3) | collective-permute-done | bytes 160 | tf_op jit(solution)/shard_map/ppermute | solution.py:193
  24.4 1.4 %collective-permute-start.2 = (s32[2,16]{1,0:T(2,128)S(1)}, s32[2,16]{1,0:T(2,128)S(1)}, u32[]{:S(2)}, u32[]{:S(2)}) collective-permute-start(s32[2,16]{1,0:T(2,128)S(1)} %bitcast.34), channel_id=1, source_target_pairs={{16,4},{17,5},{18,6},{19,7},{20,0},{21,1},{22,2},{23,3},{24,12},{2... | collective-permute-start | bytes 392 | tf_op jit(solution)/shard_map/ppermute | solution.py:193
  25.8 2.4 %collective-permute-done.2.refs_2_ = s32[2,16]{1,0:T(2,128)S(1)} collective-permute-done((s32[2,16]{1,0:T(2,128)S(1)}, s32[2,16]{1,0:T(2,128)S(1)}, u32[]{:S(2)}, u32[]{:S(2)}) %collective-permute-start.2) | collective-permute-done | bytes 160 | tf_op jit(solution)/shard_map/ppermute | solution.py:193
  28.2 0.0 copy-done
  28.2 2.0 %list.1 = (s32[138]{0:T(256)S(1)}, f32[1024,128]{1,0:T(8,128)S(1)}) custom-call(s32[4,8]{1,0:T(4,128)S(1)} %bitcast.32, s32[2,8]{1,0:T(2,128)S(1)} %collective-permute-done.refs_0_, s32[2,8]{1,0:T(2,128)S(1)} %collective-permute-done.1.refs_1_, s32[2,16]{1,0:T(2,128)S(1)} %collective-permute-done.2.refs_2_, s32[2,16]{1,0:T(2,128)S(1)} %collective-permute-done.3.refs_3_, ...), custom_call_target="tpu_custom_call" | custom-call | bytes 1000000 | tf_op jit(solution)/shard_map/list/pallas_call | solution.py:195
  30.2 0.0 collective-permute-done.5
  30.2 0.0 collective-permute-done.4
  30.3 0.0 collective-permute-done.7
  30.3 0.0 collective-permute-done.6
  30.3 0.8 %products.1 = f32[1024,128]{1,0:T(8,128)S(1)} custom-call(s32[138]{0:T(256)S(1)} %get-tuple-element.7.entries, f32[512,128]{1,0:T(8,128)S(1)} %bitcast.31, f32[512,128]{1,0:T(8,128)S(1)} %bitcast.30, f32[1024,128]{1,0:T(8,128)S(1)} %bitcast.29, f32[1024,128]{1,0:T(8,128)S(1)} %bitcast.28, ...), custom_call_target="tpu_custom_call", output_to_operand_aliasing={{}: (5, {})} | custom-call | flops 100000000 | bytes 2000000 | tf_op jit(solution)/shard_map/products/pallas_call | solution.py:204
  31.1 0.7 %collective-permute-start.8 = (f32[1024,128]{1,0:T(8,128)S(1)}, f32[1024,128]{1,0:T(8,128)S(1)}, u32[]{:S(2)}, u32[]{:S(2)}) collective-permute-start(f32[1024,128]{1,0:T(8,128)S(1)} %products.1), channel_id=1, source_target_pairs={{0,16},{16,0},{1,17},{17,1},{2,18},{18,2},{3,19},{19,3},{4,20},{20... | collective-permute-start | bytes 1572872 | tf_op jit(solution)/shard_map/ppermute | solution.py:215
  31.8 1.5 %collective-permute-done.8 = f32[1024,128]{1,0:T(8,128)S(1)} collective-permute-done((f32[1024,128]{1,0:T(8,128)S(1)}, f32[1024,128]{1,0:T(8,128)S(1)}, u32[]{:S(2)}, u32[]{:S(2)}) %collective-permute-start.8) | collective-permute-done | bytes 524320 | tf_op jit(solution)/shard_map/ppermute | solution.py:215
  33.4 0.8 %add.3 = f32[1024,128]{1,0:T(8,128)} add(f32[1024,128]{1,0:T(8,128)S(1)} %products.1, f32[1024,128]{1,0:T(8,128)S(1)} %collective-permute-done.8) | non-fusion elementwise | flops 131072 | bytes 1572864 | tf_op jit(solution)/shard_map/add | solution.py:216
  (3 shorter events, 0.0 us)
Async XLA Ops:
  0.0 7.5 %copy-start.2 = (s32[8,2]{0,1:T(2,128)S(1)}, s32[8,2]{0,1:T(2,128)}, u32[]{:S(2)}) copy-start(s32[8,2]{0,1:T(2,128)} %param.6) | copy-start | bytes 196
  0.0 30.3 %collective-permute-start.7 = (f32[16,2,4096]{2,1,0:T(2,128)}, f32[16,2,4096]{2,1,0:T(2,128)S(1)}, u32[]{:S(2)}, u32[]{:S(2)}) collective-permute-start(f32[16,2,4096]{2,1,0:T(2,128)} %param.7), channel_id=1, source_target_pairs={{0,28},{1,29},{2,30},{3,31},{4,24},{5,25},{6,26},{7,27},{8,20},{9,... | collective-permute-start | bytes 1572872 | tf_op jit(solution)/shard_map/ppermute | solution.py:191
  3.4 26.9 %collective-permute-start.6 = (f32[16,2,4096]{2,1,0:T(2,128)}, f32[16,2,4096]{2,1,0:T(2,128)S(1)}, u32[]{:S(2)}, u32[]{:S(2)}) collective-permute-start(f32[16,2,4096]{2,1,0:T(2,128)} %param.7), channel_id=1, source_target_pairs={{0,4},{1,5},{2,6},{3,7},{4,0},{5,1},{6,2},{7,3},{8,12},{9,13},{10,... | collective-permute-start | bytes 1572872 | tf_op jit(solution)/shard_map/ppermute | solution.py:191
  3.9 26.3 %collective-permute-start.5 = (f32[8,2,4096]{2,1,0:T(2,128)}, f32[8,2,4096]{2,1,0:T(2,128)S(1)}, u32[]{:S(2)}, u32[]{:S(2)}) collective-permute-start(f32[8,2,4096]{2,1,0:T(2,128)} %param.5), channel_id=1, source_target_pairs={{0,3},{16,0},{18,17},{2,18},{1,2},{17,1},{19,16},{3,19},{4,7},{20,... | collective-permute-start | bytes 786440 | tf_op jit(solution)/shard_map/ppermute | solution.py:192
  7.5 22.7 %collective-permute-start.4 = (f32[8,2,4096]{2,1,0:T(2,128)}, f32[8,2,4096]{2,1,0:T(2,128)S(1)}, u32[]{:S(2)}, u32[]{:S(2)}) collective-permute-start(f32[8,2,4096]{2,1,0:T(2,128)} %param.5), channel_id=1, source_target_pairs={{16,2},{0,1},{2,16},{18,19},{17,3},{1,0},{3,17},{19,18},{20,6},{4,... | collective-permute-start | bytes 786440 | tf_op jit(solution)/shard_map/ppermute | solution.py:192
  7.5 13.3 %copy-start.1 = (s32[16,2]{0,1:T(2,128)S(1)}, s32[16,2]{0,1:T(2,128)}, u32[]{:S(2)}) copy-start(s32[16,2]{0,1:T(2,128)} %param.8) | copy-start | bytes 388
  7.5 20.7 %copy-start = (s32[8,4]{0,1:T(4,128)S(1)}, s32[8,4]{0,1:T(4,128)}, u32[]{:S(2)}) copy-start(s32[8,4]{0,1:T(4,128)} %param.9) | copy-start | bytes 388
  7.5 8.3 %collective-permute-start.1 = (s32[2,8]{1,0:T(2,128)S(1)}, s32[2,8]{1,0:T(2,128)S(1)}, u32[]{:S(2)}, u32[]{:S(2)}) collective-permute-start(s32[2,8]{1,0:T(2,128)S(1)} %bitcast.36), channel_id=1, source_target_pairs={{0,3},{16,0},{18,17},{2,18},{1,2},{17,1},{19,16},{3,19},{4,7},{20,... | collective-permute-start | bytes 200 | tf_op jit(solution)/shard_map/ppermute | solution.py:194
  15.8 5.0 %collective-permute-start = (s32[2,8]{1,0:T(2,128)S(1)}, s32[2,8]{1,0:T(2,128)S(1)}, u32[]{:S(2)}, u32[]{:S(2)}) collective-permute-start(s32[2,8]{1,0:T(2,128)S(1)} %bitcast.37), channel_id=1, source_target_pairs={{16,2},{0,1},{2,16},{18,19},{17,3},{1,0},{3,17},{19,18},{20,6},{4,... | collective-permute-start | bytes 200 | tf_op jit(solution)/shard_map/ppermute | solution.py:194
  20.8 3.6 %collective-permute-start.3 = (s32[2,16]{1,0:T(2,128)S(1)}, s32[2,16]{1,0:T(2,128)S(1)}, u32[]{:S(2)}, u32[]{:S(2)}) collective-permute-start(s32[2,16]{1,0:T(2,128)S(1)} %bitcast.33), channel_id=1, source_target_pairs={{0,8},{1,9},{2,10},{3,11},{4,12},{5,13},{6,14},{7,15},{8,0},{9,1},... | collective-permute-start | bytes 392 | tf_op jit(solution)/shard_map/ppermute | solution.py:193
  24.4 3.8 %collective-permute-start.2 = (s32[2,16]{1,0:T(2,128)S(1)}, s32[2,16]{1,0:T(2,128)S(1)}, u32[]{:S(2)}, u32[]{:S(2)}) collective-permute-start(s32[2,16]{1,0:T(2,128)S(1)} %bitcast.34), channel_id=1, source_target_pairs={{16,4},{17,5},{18,6},{19,7},{20,0},{21,1},{22,2},{23,3},{24,12},{2... | collective-permute-start | bytes 392 | tf_op jit(solution)/shard_map/ppermute | solution.py:193
  31.1 2.3 %collective-permute-start.8 = (f32[1024,128]{1,0:T(8,128)S(1)}, f32[1024,128]{1,0:T(8,128)S(1)}, u32[]{:S(2)}, u32[]{:S(2)}) collective-permute-start(f32[1024,128]{1,0:T(8,128)S(1)} %products.1), channel_id=1, source_target_pairs={{0,16},{16,0},{1,17},{17,1},{2,18},{18,2},{3,19},{19,3},{4,20},{20... | collective-permute-start | bytes 1572872 | tf_op jit(solution)/shard_map/ppermute | solution.py:215
